TPU v7x, 32 devices: a whole 2x2x4 slice. The times are simulated.
32 devices in a mesh: groups: 2 (over y), rows: 4 (over z), cols: 4 (over x, core).
Axes of the slice: x: 2, y: 2, z: 4, core: 2. Of those that a mesh axis runs over, the one named last changes fastest.
Arguments:
- tokens: bfloat16 [128, 256, 512], P(('groups', 'rows'), 'cols'), parts along dimension 0, may hold values from -30 to 30
- qkv_weight: bfloat16 [512, 1536], replicated, may hold values from -0.25 to 0.25
- depth_kernel: float32 [25, 1536], replicated, may hold values from -1.25 to 1.25
- group_kernel: bfloat16 [48, 32, 32], replicated, may hold values from -1 to 1
- proj_weight: bfloat16 [1024, 512], replicated, may hold values from -0.1875 to 0.1875
- out_gain: float32 [512], replicated, may hold values from 4 to 16
- out_bias: float32 [512], replicated, may hold values from -3 to 3
Outputs:
- output: bfloat16 [128, 256, 512], P(('groups', 'rows'), 'cols'), parts along dimension 0
There are 2 independent parts, one for each index of `groups`. A program takes and returns all parts, laid end to end along the dimension named above; an argument that names none is the same for every part. Nothing has to cross between parts.
All inputs are finite; a program needn't handle non-finite values.
Results may differ from a plain program's by a relative error of at most 0.0048.
Values may be sent and summed in bfloat16 or wider, within the bound.
A program may use at most 64 MiB of HBM per device.

v0:
```python
import jax
import jax.numpy as jnp
from jax import lax
from jax.sharding import PartitionSpec as P

HEAD_DIM = 32


def padded_2(value, sides, width):
    for axis, dim in sides:
        size, length = (lax.axis_size(axis), value.shape[dim])
        up = [(i, (i + 1) % size) for i in range(size - 1)]
        down = [(j, i) for i, j in up]
        last = lax.slice_in_dim(value, length - width, length, axis=dim)
        leading = lax.slice_in_dim(value, 0, width, axis=dim)
        before = lax.ppermute(last, axis, up)
        after = lax.ppermute(leading, axis, down)
        value = jnp.concatenate([before, value, after], axis=dim)
    return value


def feature_map(inputs):
    return jax.nn.elu(inputs.astype(jnp.float32)) + 1.0


def aggregate(padded, depth_kernel, group_kernel, height, breadth):
    channels = padded.shape[2]
    summed = jnp.zeros((height, breadth, channels), jnp.float32)
    for offset_row in range(5):
        for offset_col in range(5):
            window = padded[offset_row : offset_row + height, offset_col : offset_col + breadth]
            summed = summed + window * depth_kernel[offset_row * 5 + offset_col]
    spread = summed.astype(jnp.bfloat16).reshape(height * breadth, channels // HEAD_DIM, HEAD_DIM)
    grouped = jnp.einsum("ngc,gcd->ngd", spread, group_kernel, preferred_element_type=jnp.float32)
    return grouped.astype(jnp.bfloat16).reshape(height * breadth, channels)


def context_states(source):
    amount = source.shape[0]
    grouped = source.reshape(amount, -1, 3, HEAD_DIM)
    key_feats = feature_map(grouped[:, :, 1]).astype(jnp.bfloat16)
    values = grouped[:, :, 2]
    states = jnp.einsum("nhd,nhe->hde", key_feats, values, preferred_element_type=jnp.float32)
    totals = jnp.sum(key_feats.astype(jnp.float32), axis=0)
    return (states, totals)


def body(tokens, qkv_weight, depth_kernel, group_kernel, proj_weight, out_gain, out_bias):
    height, breadth, channels = tokens.shape
    amount = height * breadth
    triple = jnp.dot(
        tokens.reshape(amount, channels), qkv_weight, preferred_element_type=jnp.float32
    )
    triple = triple.astype(jnp.bfloat16).reshape(height, breadth, 3 * channels)
    padded = padded_2(triple, (("rows", 0), ("cols", 1)), 2)
    flat_triple = triple.reshape(amount, 3 * channels)
    plain_state, plain_total = context_states(flat_triple)
    aggregated = aggregate(padded, depth_kernel, group_kernel, height, breadth)
    scaled_state, scaled_total = context_states(aggregated)
    states, totals = lax.psum(
        (
            jnp.concatenate([plain_state, scaled_state], 0),
            jnp.concatenate([plain_total, scaled_total], 0),
        ),
        ("rows", "cols"),
    )
    queries = jnp.concatenate(
        [
            feature_map(flat_triple.reshape(amount, -1, 3, HEAD_DIM)[:, :, 0]),
            feature_map(aggregated.reshape(amount, -1, 3, HEAD_DIM)[:, :, 0]),
        ],
        1,
    )
    numerator = jnp.einsum("nhd,hde->nhe", queries, states, precision=lax.Precision.HIGHEST)
    denominator = jnp.einsum("nhd,hd->nh", queries, totals, precision=lax.Precision.HIGHEST)
    attended = (
        (numerator / denominator[:, :, None]).astype(jnp.bfloat16).reshape(amount, 2 * channels)
    )
    projected = jnp.dot(attended, proj_weight, preferred_element_type=jnp.float32)
    result = tokens.reshape(amount, channels).astype(jnp.float32) + out_gain * projected + out_bias
    return result.astype(jnp.bfloat16).reshape(height, breadth, channels)


def solution(mesh):
    placed = (P(("groups", "rows"), "cols", None), P(), P(), P(), P(), P(), P())
    return jax.shard_map(
        body,
        mesh=mesh,
        in_specs=placed,
        out_specs=P(("groups", "rows"), "cols", None),
        check_vma=False,
    )
```

profile of v0, /device:TPU:1, one launch (start us, length us, event | category | flops | bytes accessed | tf_op | source)
XLA Modules:
  0.0 203.0 jit_solution(8702821918944475526)
XLA Ops:
  6.5 1.4 copy-done
  7.9 3.0 %convolution_convert_fusion = bf16[1024,1536]{1,0:T(8,128)(2,1)S(1)} fusion(bf16[1024,512]{1,0:T(8,128)(2,1)} %bitcast.85, bf16[512,1536]{1,0:T(8,128)(2,1)S(1)} %copy-done), kind=kOutput, calls=%fused_computation.14 | convolution fusion | flops 1612185600 | bytes 5767168 | tf_op jit(solution)/shard_map/dot_general | solution.py:51
  11.0 1.7 copy-done.1
  12.6 0.1 fusion.25
  12.7 4.1 %collective-permute-start = (bf16[2,64,1536]{2,1,0:T(8,128)(2,1)S(1)}, bf16[2,64,1536]{2,1,0:T(8,128)(2,1)S(1)}, u32[]{:S(2)}, u32[]{:S(2)}) collective-permute-start(bf16[2,64,1536]{2,1,0:T(8,128)(2,1)S(1)} %bitcast.82), channel_id=1, source_target_pairs={{0,4},{4,8},{8,12},{1,5},{5,9},{9,13},{2,6},{6,10},{10,14},{3,7},{... | collective-permute-start | bytes 1179656 | tf_op jit(solution)/shard_map/ppermute | solution.py:16
  16.7 1.3 collective-permute-start.1
  18.0 4.7 %copy.26 = bf16[1024,1536]{0,1:T(8,128)(2,1)} copy(bf16[1024,1536]{1,0:T(8,128)(2,1)} %copy-done.1) | data formatting | bytes 6291456 | tf_op jit(solution)/shard_map/convert_element_type | solution.py:54
  22.8 3.5 %fusion.16 = f32[16,32,32]{2,1,0:T(8,128)} fusion(bf16[1024,16,3,32]{0,3,2,1:T(8,128)(2,1)} %bitcast.77), kind=kOutput, calls=%fused_computation.45 | convolution fusion | flops 36700160 | bytes 2162688 | tf_op jit(solution)/shard_map/nhd,nhe->hde/dot_general | solution.py:43
  26.3 0.0 collective-permute-done
  26.3 2.0 %collective-permute-done.1 = bf16[2,64,1536]{2,1,0:T(8,128)(2,1)S(1)} collective-permute-done((bf16[2,64,1536]{2,1,0:T(8,128)(2,1)S(1)}, bf16[2,64,1536]{2,1,0:T(8,128)(2,1)S(1)}, u32[]{:S(2)}, u32[]{:S(2)}) %collective-permute-start.1) | collective-permute-done | bytes 393248 | tf_op jit(solution)/shard_map/ppermute | solution.py:17
  28.3 0.2 pad_maximum_fusion.11
  28.5 4.9 %collective-permute-start.2 = (bf16[20,2,1536]{2,1,0:T(2,128)(2,1)S(1)}, bf16[20,2,1536]{2,1,0:T(2,128)(2,1)S(1)}, u32[]{:S(2)}, u32[]{:S(2)}) collective-permute-start(bf16[20,2,1536]{2,1,0:T(2,128)(2,1)S(1)} %get-tuple-element.32), channel_id=1, source_target_pairs={{0,1},{1,2},{2,3},{4,5},{5,6},{6,7},{8,9},{9,10},{10,11},{12,13},{... | collective-permute-start | bytes 368648 | tf_op jit(solution)/shard_map/ppermute | solution.py:16
  33.4 2.1 %collective-permute-start.3 = (bf16[20,2,1536]{2,1,0:T(2,128)(2,1)S(1)}, bf16[20,2,1536]{2,1,0:T(2,128)(2,1)S(1)}, u32[]{:S(2)}, u32[]{:S(2)}) collective-permute-start(bf16[20,2,1536]{2,1,0:T(2,128)(2,1)S(1)} %get-tuple-element.33), channel_id=1, source_target_pairs={{1,0},{2,1},{3,2},{5,4},{6,5},{7,6},{9,8},{10,9},{11,10},{13,12},{... | collective-permute-start | bytes 368648 | tf_op jit(solution)/shard_map/ppermute | solution.py:17
  35.5 0.9 slice_reduce_fusion.24
  36.4 0.7 copy.29
  37.1 1.1 slice_reduce_fusion.23
  38.3 1.2 collective-permute-done.3
  39.6 5.1 %maximum_maximum_fusion = (bf16[20,66,1536]{2,1,0:T(8,128)(2,1)S(1)}, bf16[20,66,1536]{2,1,0:T(8,128)(2,1)S(1)}) fusion(bf16[2,64,1536]{2,1,0:T(8,128)(2,1)S(1)} %collective-permute-done.1, bf16[16,64,1536]{2,1,0:T(8,128)(2,1)} %bitcast.74, bf16[2,64,1536]{2,1,0:T(8,128)(2,1)S(1)} %collective-permute-done, ...), kind=kLoop, calls=%fused_computation.9 | loop fusion | flops 32440320 | bytes 12288000 | tf_op jit(solution)/shard_map/concatenate | solution.py:18
  44.9 24.0 %add_convert_fusion = bf16[16,64,1536]{2,1,0:T(8,128)(2,1)} fusion(bf16[16,64,1536]{2,1,0:T(8,128)(2,1)S(1)} %bitcast.76, bf16[2,64,1536]{2,1,0:T(8,128)(2,1)S(1)} %collective-permute-done.1, bf16[2,64,1536]{2,1,0:T(8,128)(2,1)S(1)} %collective-permute-done, bf16[20,66,1536]{2,1,0:T(8,128)(2,1)S(1)} %get-tuple-element.31, ...), kind=kLoop, calls=%fused_computation.8 | loop fusion | flops 124256256 | bytes 70146048 | tf_op jit(solution)/shard_map/convert_element_type | solution.py:33
  68.9 8.6 %copy.28 = bf16[16,64,1536]{1,0,2:T(8,128)(2,1)} copy(bf16[16,64,1536]{2,1,0:T(8,128)(2,1)} %add_convert_fusion) | data formatting | bytes 6291456 | tf_op jit(solution)/shard_map/convert_element_type | solution.py:33
  77.5 9.4 %reshape.56 = bf16[1024,48,32]{0,2,1:T(8,128)(2,1)} reshape(bf16[16,64,1536]{1,0,2:T(8,128)(2,1)} %copy.28) | data formatting | bytes 6291456 | tf_op jit(solution)/shard_map/reshape | solution.py:33
  86.9 2.8 %convolution_convert_fusion.1 = bf16[48,1024,32]{1,2,0:T(8,128)(2,1)S(1)} fusion(bf16[48,32,32]{1,2,0:T(8,128)(2,1)S(1)} %copy.29, bf16[1024,48,32]{0,2,1:T(8,128)(2,1)} %reshape.56), kind=kOutput, calls=%fused_computation.25 | convolution fusion | flops 102236160 | bytes 6389760 | tf_op jit(solution)/shard_map/ngc,gcd->ngd/dot_general | solution.py:34
  89.7 1.1 fusion.15
  90.8 0.8 copy-done.4
  91.6 5.6 %fusion.12 = (f32[1024,16,32]{0,2,1:T(8,128)}, f32[16,32]{1,0:T(8,128)S(1)}, f32[16,32]{1,0:T(8,128)S(1)}, f32[1024,16,32]{0,2,1:T(8,128)}) fusion(bf16[1024,16,3,32]{0,3,2,1:T(8,128)(2,1)S(1)} %bitcast.78, bf16[1024,16,3,32]{0,3,2,1:T(8,128)(2,1)S(1)} %bitcast.80), kind=kLoop, calls=%fused_computation.33 | loop fusion | flops 13630464 | bytes 8392704 | tf_op jit(solution)/shard_map/add | solution.py:23
  97.2 0.8 pad_maximum_fusion.8
  98.0 0.0 all-reduce.2.cloned.1.call-update
  98.1 53.2 %psum.15 = f32[32,32]{1,0:T(8,128)S(1)} all-reduce(f32[32,32]{1,0:T(8,128)S(1)} %pad_maximum_fusion.12), channel_id=1, replica_groups=mesh['groups'=2,'rows'=4,'cols'=4] {'rows','cols'}, use_global_device_ids=true, to_apply=%region_3.4 | all-reduce | flops 1024 | bytes 8192 | tf_op jit(solution)/shard_map/psum | solution.py:60
  151.3 4.3 %fusion.1 = f32[32,1,1024]{2,1,0:T(1,128)S(1)} fusion(f32[32,32,1]{1,2,0:T(1,128)S(1)} %bitcast.84, f32[1024,16,32]{0,2,1:T(8,128)} %get-tuple-element.41, f32[1024,16,32]{0,2,1:T(8,128)} %get-tuple-element.34), kind=kOutput, calls=%fused_computation.19 | convolution fusion | flops 13631488 | bytes 4329472 | tf_op jit(solution)/shard_map/nhd,hd->nh/dot_general | solution.py:75
  155.6 32.5 %all-reduce.2.cloned.1.call-done = f32[32,32,32]{2,1,0:T(8,128)} async-done(((f32[32,32,32]{2,1,0:T(8,128)}), f32[32,32,32]{2,1,0:T(8,128)}) %all-reduce.2.cloned.1.call-update) | async-done | bytes 131088 | tf_op jit(solution)/shard_map/psum | solution.py:60
  188.1 5.7 %fusion = bf16[1024,32,32]{0,2,1:T(8,128)(2,1)S(1)} fusion(f32[1024,32]{0,1:T(8,128)S(1)} %bitcast.83, f32[32,32,32]{2,1,0:T(8,128)} %all-reduce.2.cloned.1.call-done, f32[1024,16,32]{0,2,1:T(8,128)} %get-tuple-element.41, f32[1024,16,32]{0,2,1:T(8,128)} %get-tuple-element.34), kind=kOutput, calls=%fused_computation.13 | convolution fusion | flops 405798912 | bytes 6553600 | tf_op jit(solution)/shard_map/nhd,hde->nhe/dot_general | solution.py:74
  193.9 2.3 %add_convert_fusion.1 = bf16[1024,512]{1,0:T(8,128)(2,1)} fusion(bf16[1024,512]{1,0:T(8,128)(2,1)S(1)} %bitcast.86, bf16[1024,1024]{0,1:T(8,128)(2,1)S(1)} %bitcast.87, bf16[1024,512]{1,0:T(8,128)(2,1)S(1)} %copy-done.22, f32[512]{0:T(512)S(1)} %copy-done.23, f32[512]{0:T(512)S(1)} %copy-done.24), kind=kOutput, calls=%fused_computation.36 | convolution fusion | flops 1076363264 | bytes 5246976 | tf_op jit(solution)/shard_map/dot_general | solution.py:79
  (51 shorter events, 0.1 us)
Async XLA Ops:
  6.5 1.4 copy-start
  6.5 181.5 %all-reduce.2.cloned.1.call-start = ((), (), s32[]{:S(2)}) async-start(), calls=%async_computation | async-start | bytes 1048576 | tf_op jit(solution)/shard_map/psum | solution.py:60
  11.0 1.7 copy-start.1
  12.7 13.6 %collective-permute-start = (bf16[2,64,1536]{2,1,0:T(8,128)(2,1)S(1)}, bf16[2,64,1536]{2,1,0:T(8,128)(2,1)S(1)}, u32[]{:S(2)}, u32[]{:S(2)}) collective-permute-start(bf16[2,64,1536]{2,1,0:T(8,128)(2,1)S(1)} %bitcast.82), channel_id=1, source_target_pairs={{0,4},{4,8},{8,12},{1,5},{5,9},{9,13},{2,6},{6,10},{10,14},{3,7},{... | collective-permute-start | bytes 1179656 | tf_op jit(solution)/shard_map/ppermute | solution.py:16
  16.7 11.6 %collective-permute-start.1 = (bf16[2,64,1536]{2,1,0:T(8,128)(2,1)S(1)}, bf16[2,64,1536]{2,1,0:T(8,128)(2,1)S(1)}, u32[]{:S(2)}, u32[]{:S(2)}) collective-permute-start(bf16[2,64,1536]{2,1,0:T(8,128)(2,1)S(1)} %bitcast.81), channel_id=1, source_target_pairs={{4,0},{8,4},{12,8},{5,1},{9,5},{13,9},{6,2},{10,6},{14,10},{7,3},{... | collective-permute-start | bytes 1179656 | tf_op jit(solution)/shard_map/ppermute | solution.py:17
  22.8 5.5 %copy-start.2 = (bf16[1024,1536]{1,0:T(8,128)(2,1)S(1)}, bf16[1024,1536]{1,0:T(8,128)(2,1)}, u32[]{:S(2)}) copy-start(bf16[1024,1536]{1,0:T(8,128)(2,1)} %copy-done.1) | copy-start | bytes 9437188
  22.8 12.7 %copy-start.7 = (f32[25,1536]{1,0:T(8,128)S(1)}, f32[25,1536]{1,0:T(8,128)}, u32[]{:S(2)}) copy-start(f32[25,1536]{1,0:T(8,128)} %param.9) | copy-start | bytes 460804
  22.8 13.6 %copy-start.5 = (bf16[48,32,32]{0,2,1:T(8,128)(2,1)S(1)}, bf16[48,32,32]{0,2,1:T(8,128)(2,1)}, u32[]{:S(2)}) copy-start(bf16[48,32,32]{0,2,1:T(8,128)(2,1)} %param.10) | copy-start | bytes 294916
  28.5 9.8 %collective-permute-start.2 = (bf16[20,2,1536]{2,1,0:T(2,128)(2,1)S(1)}, bf16[20,2,1536]{2,1,0:T(2,128)(2,1)S(1)}, u32[]{:S(2)}, u32[]{:S(2)}) collective-permute-start(bf16[20,2,1536]{2,1,0:T(2,128)(2,1)S(1)} %get-tuple-element.32), channel_id=1, source_target_pairs={{0,1},{1,2},{2,3},{4,5},{5,6},{6,7},{8,9},{9,10},{10,11},{12,13},{... | collective-permute-start | bytes 368648 | tf_op jit(solution)/shard_map/ppermute | solution.py:16
  33.4 6.2 %collective-permute-start.3 = (bf16[20,2,1536]{2,1,0:T(2,128)(2,1)S(1)}, bf16[20,2,1536]{2,1,0:T(2,128)(2,1)S(1)}, u32[]{:S(2)}, u32[]{:S(2)}) collective-permute-start(bf16[20,2,1536]{2,1,0:T(2,128)(2,1)S(1)} %get-tuple-element.33), channel_id=1, source_target_pairs={{1,0},{2,1},{3,2},{5,4},{6,5},{7,6},{9,8},{10,9},{11,10},{13,12},{... | collective-permute-start | bytes 368648 | tf_op jit(solution)/shard_map/ppermute | solution.py:17
  38.2 6.5 %copy-start.3 = (bf16[1024,1536]{1,0:T(8,128)(2,1)S(1)}, bf16[1024,1536]{1,0:T(8,128)(2,1)}, u32[]{:S(2)}) copy-start(bf16[1024,1536]{1,0:T(8,128)(2,1)} %copy-done.1) | copy-start | bytes 9437188
  38.2 6.5 %copy-start.8 = (f32[1536]{0:T(1024)S(1)}, f32[1536]{0:T(1024)}, u32[]{:S(2)}) copy-start(f32[1536]{0:T(1024)} %get-tuple-element.11) | copy-start | bytes 18436
  38.2 6.5 %copy-start.9 = (f32[1536]{0:T(1024)S(1)}, f32[1536]{0:T(1024)}, u32[]{:S(2)}) copy-start(f32[1536]{0:T(1024)} %get-tuple-element.12) | copy-start | bytes 18436
  38.2 6.5 %copy-start.10 = (f32[1536]{0:T(1024)S(1)}, f32[1536]{0:T(1024)}, u32[]{:S(2)}) copy-start(f32[1536]{0:T(1024)} %get-tuple-element.13) | copy-start | bytes 18436
  38.2 6.5 %copy-start.11 = (f32[1536]{0:T(1024)S(1)}, f32[1536]{0:T(1024)}, u32[]{:S(2)}) copy-start(f32[1536]{0:T(1024)} %get-tuple-element.14) | copy-start | bytes 18436
  38.2 6.5 %copy-start.12 = (f32[1536]{0:T(1024)S(1)}, f32[1536]{0:T(1024)}, u32[]{:S(2)}) copy-start(f32[1536]{0:T(1024)} %get-tuple-element.15) | copy-start | bytes 18436
  38.2 6.5 %copy-start.13 = (f32[1536]{0:T(1024)S(1)}, f32[1536]{0:T(1024)}, u32[]{:S(2)}) copy-start(f32[1536]{0:T(1024)} %get-tuple-element.16) | copy-start | bytes 18436
  38.3 6.5 %copy-start.14 = (f32[1536]{0:T(1024)S(1)}, f32[1536]{0:T(1024)}, u32[]{:S(2)}) copy-start(f32[1536]{0:T(1024)} %get-tuple-element.17) | copy-start | bytes 18436
  38.3 6.5 %copy-start.15 = (f32[1536]{0:T(1024)S(1)}, f32[1536]{0:T(1024)}, u32[]{:S(2)}) copy-start(f32[1536]{0:T(1024)} %get-tuple-element.18) | copy-start | bytes 18436
  38.3 6.5 %copy-start.16 = (f32[1536]{0:T(1024)S(1)}, f32[1536]{0:T(1024)}, u32[]{:S(2)}) copy-start(f32[1536]{0:T(1024)} %get-tuple-element.19) | copy-start | bytes 18436
  38.3 6.5 %copy-start.17 = (f32[1536]{0:T(1024)S(1)}, f32[1536]{0:T(1024)}, u32[]{:S(2)}) copy-start(f32[1536]{0:T(1024)} %get-tuple-element.20) | copy-start | bytes 18436
  38.3 6.5 %copy-start.18 = (f32[1536]{0:T(1024)S(1)}, f32[1536]{0:T(1024)}, u32[]{:S(2)}) copy-start(f32[1536]{0:T(1024)} %get-tuple-element.21) | copy-start | bytes 18436
  38.3 6.5 %copy-start.19 = (f32[1536]{0:T(1024)S(1)}, f32[1536]{0:T(1024)}, u32[]{:S(2)}) copy-start(f32[1536]{0:T(1024)} %get-tuple-element.22) | copy-start | bytes 18436
  38.3 6.5 %copy-start.20 = (f32[1536]{0:T(1024)S(1)}, f32[1536]{0:T(1024)}, u32[]{:S(2)}) copy-start(f32[1536]{0:T(1024)} %get-tuple-element.23) | copy-start | bytes 18436
  89.7 1.9 copy-start.4
  91.6 5.6 %copy-start.6 = (f32[16,32,32]{2,1,0:T(8,128)S(1)}, f32[16,32,32]{2,1,0:T(8,128)}, u32[]{:S(2)}) copy-start(f32[16,32,32]{2,1,0:T(8,128)} %fusion.16) | copy-start | bytes 196612
  188.1 5.8 %copy-start.21 = (bf16[16,64,512]{2,1,0:T(8,128)(2,1)S(1)}, bf16[16,64,512]{2,1,0:T(8,128)(2,1)}, u32[]{:S(2)}) copy-start(bf16[16,64,512]{2,1,0:T(8,128)(2,1)} %param.7) | copy-start | bytes 3145732
  188.1 5.8 %copy-start.22 = (bf16[1024,512]{1,0:T(8,128)(2,1)S(1)}, bf16[1024,512]{1,0:T(8,128)(2,1)}, u32[]{:S(2)}) copy-start(bf16[1024,512]{1,0:T(8,128)(2,1)} %param.11) | copy-start | bytes 3145732
  188.1 5.8 %copy-start.23 = (f32[512]{0:T(512)S(1)}, f32[512]{0:T(512)}, u32[]{:S(2)}) copy-start(f32[512]{0:T(512)} %param.13) | copy-start | bytes 6148
  188.1 5.8 %copy-start.24 = (f32[512]{0:T(512)S(1)}, f32[512]{0:T(512)}, u32[]{:S(2)}) copy-start(f32[512]{0:T(512)} %param.12) | copy-start | bytes 6148
Sparse Core Ops, SparseCore 0:
  98.2 89.8 all-reduce.1
where the time goes:
time: 204 us; the launch traced here: 203 us
  blocking collectives  53.2 us (26%)
  waiting for transfers between devices  35.8 us (18%)
  other arithmetic  35.8 us (18%)
  local copies, waits for them, and re-layouts  29.4 us (14%)
  matrix products  22.8 us (11%)
  between operations  13.8 us (7%)
  starting transfers between devices  12.3 us (6%)
    psum x1, blocking collectives, body(): lax.psum((jnp.concatenate([plain_state, scaled_state], 0), jnp.concatenat...  53.2 us
    psum x1, waiting for transfers between devices, body(): lax.psum((jnp.concatenate([plain_state, scaled_state], 0), jnp.concatenat...  32.5 us
    convert_element_type x1, other arithmetic, aggregate(): summed.astype(jnp.bfloat16)  24 us
    reshape x1, local copies, waits for them, and re-layouts, aggregate(): summed.astype(jnp.bfloat16)  9.4 us
    ppermute x2, starting transfers between devices, padded_2(): before = lax.ppermute(last, axis, up)  8.92 us
    convert_element_type x1, local copies, waits for them, and re-layouts, aggregate(): summed.astype(jnp.bfloat16)  8.57 us
    dot_general x1, matrix products, body(): jnp.einsum('nhd,hde->nhe', queries, states, precision=lax.Precision.HIGHEST)  5.75 us
    add x1, other arithmetic, feature_map(): return jax.nn.elu(inputs.astype(jnp.float32)) + 1.0  5.57 us
  transfers between devices with their start and end apart: 5, of which 3 were waited for; matrix products, arithmetic and copies ran while one was open for 8% of the time, Pallas kernels for 0%

commit v1 on v0

--- a/solution.py
+++ b/solution.py
@@ -58,11 +58,14 @@
     aggregated = aggregate(padded, depth_kernel, group_kernel, height, breadth)
     scaled_state, scaled_total = context_states(aggregated)
     states, totals = lax.psum(
-        (
-            jnp.concatenate([plain_state, scaled_state], 0),
-            jnp.concatenate([plain_total, scaled_total], 0),
+        lax.psum(
+            (
+                jnp.concatenate([plain_state, scaled_state], 0),
+                jnp.concatenate([plain_total, scaled_total], 0),
+            ),
+            axis_name="cols",
         ),
-        ("rows", "cols"),
+        axis_name="rows",
     )
     queries = jnp.concatenate(
         [

time: 204 us -> 188 us (0.922)
  blocking collectives: 53.2 us -> 23.3 us
  waiting for transfers between devices: 35.8 us -> 47.8 us
    psum x1, blocking collectives: 53.2 us -> 9.47 us  [body(): lax.psum((jnp.concatenate([plain_state, scaled_state], 0), jnp.concatenat...]
    psum x0 -> x1, waiting for transfers between devices: none -> 36.8 us  [body(): lax.psum(lax.psum((jnp.concatenate([plain_state, scaled_state], 0), jnp.c...]
    psum x1, waiting for transfers between devices: 32.5 us -> 7.72 us  [body(): lax.psum((jnp.concatenate([plain_state, scaled_state], 0), jnp.concatenat...]
    psum x0 -> x1, blocking collectives: none -> 13.8 us  [body(): lax.psum(lax.psum((jnp.concatenate([plain_state, scaled_state], 0), jnp.c...]
  transfers between devices with their start and end apart: 5 -> 6, of which waited for: 3 -> 4; matrix products, arithmetic and copies ran while one was open for 8% -> 8% of each run, Pallas kernels for 0% -> 0%
where the time goes in v1:
time: 188 us; the launch traced here: 185 us
  waiting for transfers between devices  47.8 us (25%)
  other arithmetic  35.8 us (19%)
  local copies, waits for them, and re-layouts  29.4 us (16%)
  blocking collectives  23.3 us (12%)
  matrix products  22.8 us (12%)
  between operations  13.8 us (7%)
  starting transfers between devices  12.4 us (7%)
    psum x1, waiting for transfers between devices, body(): lax.psum(lax.psum((jnp.concatenate([plain_state, scaled_state], 0), jnp.c...  36.8 us
    convert_element_type x1, other arithmetic, aggregate(): summed.astype(jnp.bfloat16)  24 us
    psum x1, blocking collectives, body(): lax.psum(lax.psum((jnp.concatenate([plain_state, scaled_state], 0), jnp.c...  13.8 us
    psum x1, blocking collectives, body(): lax.psum((jnp.concatenate([plain_state, scaled_state], 0), jnp.concatenat...  9.47 us
    reshape x1, local copies, waits for them, and re-layouts, aggregate(): summed.astype(jnp.bfloat16)  9.4 us
    ppermute x2, starting transfers between devices, padded_2(): before = lax.ppermute(last, axis, up)  8.92 us
    convert_element_type x1, local copies, waits for them, and re-layouts, aggregate(): summed.astype(jnp.bfloat16)  8.57 us
    psum x1, waiting for transfers between devices, body(): lax.psum((jnp.concatenate([plain_state, scaled_state], 0), jnp.concatenat...  7.72 us
  transfers between devices with their start and end apart: 6, of which 4 were waited for; matrix products, arithmetic and copies ran while one was open for 8% of the time, Pallas kernels for 0%

profile of v1, /device:TPU:1, one launch (start us, length us, event | category | flops | bytes accessed | tf_op | source)
XLA Modules:
  0.0 185.2 jit_solution(4748742970227432566)
XLA Ops:
  6.5 1.4 copy-done
  7.9 3.0 %convolution_convert_fusion = bf16[1024,1536]{1,0:T(8,128)(2,1)S(1)} fusion(bf16[1024,512]{1,0:T(8,128)(2,1)} %bitcast.85, bf16[512,1536]{1,0:T(8,128)(2,1)S(1)} %copy-done), kind=kOutput, calls=%fused_computation.14 | convolution fusion | flops 1612185600 | bytes 5767168 | tf_op jit(solution)/shard_map/dot_general | solution.py:51
  11.0 1.7 copy-done.1
  12.6 0.1 fusion.25
  12.7 4.1 %collective-permute-start = (bf16[2,64,1536]{2,1,0:T(8,128)(2,1)S(1)}, bf16[2,64,1536]{2,1,0:T(8,128)(2,1)S(1)}, u32[]{:S(2)}, u32[]{:S(2)}) collective-permute-start(bf16[2,64,1536]{2,1,0:T(8,128)(2,1)S(1)} %bitcast.82), channel_id=1, source_target_pairs={{0,4},{4,8},{8,12},{1,5},{5,9},{9,13},{2,6},{6,10},{10,14},{3,7},{... | collective-permute-start | bytes 1179656 | tf_op jit(solution)/shard_map/ppermute | solution.py:16
  16.7 1.3 collective-permute-start.1
  18.0 4.7 %copy.26 = bf16[1024,1536]{0,1:T(8,128)(2,1)} copy(bf16[1024,1536]{1,0:T(8,128)(2,1)} %copy-done.1) | data formatting | bytes 6291456 | tf_op jit(solution)/shard_map/convert_element_type | solution.py:54
  22.8 3.5 %fusion.16 = f32[16,32,32]{2,1,0:T(8,128)} fusion(bf16[1024,16,3,32]{0,3,2,1:T(8,128)(2,1)} %bitcast.77), kind=kOutput, calls=%fused_computation.45 | convolution fusion | flops 36700160 | bytes 2162688 | tf_op jit(solution)/shard_map/nhd,nhe->hde/dot_general | solution.py:43
  26.3 2.0 %collective-permute-done.1 = bf16[2,64,1536]{2,1,0:T(8,128)(2,1)S(1)} collective-permute-done((bf16[2,64,1536]{2,1,0:T(8,128)(2,1)S(1)}, bf16[2,64,1536]{2,1,0:T(8,128)(2,1)S(1)}, u32[]{:S(2)}, u32[]{:S(2)}) %collective-permute-start.1) | collective-permute-done | bytes 393248 | tf_op jit(solution)/shard_map/ppermute | solution.py:17
  28.3 0.2 pad_maximum_fusion.11
  28.5 4.9 %collective-permute-start.2 = (bf16[20,2,1536]{2,1,0:T(2,128)(2,1)S(1)}, bf16[20,2,1536]{2,1,0:T(2,128)(2,1)S(1)}, u32[]{:S(2)}, u32[]{:S(2)}) collective-permute-start(bf16[20,2,1536]{2,1,0:T(2,128)(2,1)S(1)} %get-tuple-element.32), channel_id=1, source_target_pairs={{0,1},{1,2},{2,3},{4,5},{5,6},{6,7},{8,9},{9,10},{10,11},{12,13},{... | collective-permute-start | bytes 368648 | tf_op jit(solution)/shard_map/ppermute | solution.py:16
  33.4 2.1 %collective-permute-start.3 = (bf16[20,2,1536]{2,1,0:T(2,128)(2,1)S(1)}, bf16[20,2,1536]{2,1,0:T(2,128)(2,1)S(1)}, u32[]{:S(2)}, u32[]{:S(2)}) collective-permute-start(bf16[20,2,1536]{2,1,0:T(2,128)(2,1)S(1)} %get-tuple-element.33), channel_id=1, source_target_pairs={{1,0},{2,1},{3,2},{5,4},{6,5},{7,6},{9,8},{10,9},{11,10},{13,12},{... | collective-permute-start | bytes 368648 | tf_op jit(solution)/shard_map/ppermute | solution.py:17
  35.5 0.9 slice_reduce_fusion.24
  36.4 0.7 copy.29
  37.1 1.1 slice_reduce_fusion.23
  38.4 1.2 collective-permute-done.3
  39.6 5.1 %maximum_maximum_fusion = (bf16[20,66,1536]{2,1,0:T(8,128)(2,1)S(1)}, bf16[20,66,1536]{2,1,0:T(8,128)(2,1)S(1)}) fusion(bf16[2,64,1536]{2,1,0:T(8,128)(2,1)S(1)} %collective-permute-done.1, bf16[16,64,1536]{2,1,0:T(8,128)(2,1)} %bitcast.74, bf16[2,64,1536]{2,1,0:T(8,128)(2,1)S(1)} %collective-permute-done, ...), kind=kLoop, calls=%fused_computation.9 | loop fusion | flops 32440320 | bytes 12288000 | tf_op jit(solution)/shard_map/concatenate | solution.py:18
  44.9 24.0 %add_convert_fusion = bf16[16,64,1536]{2,1,0:T(8,128)(2,1)} fusion(bf16[16,64,1536]{2,1,0:T(8,128)(2,1)S(1)} %bitcast.76, bf16[2,64,1536]{2,1,0:T(8,128)(2,1)S(1)} %collective-permute-done.1, bf16[2,64,1536]{2,1,0:T(8,128)(2,1)S(1)} %collective-permute-done, bf16[20,66,1536]{2,1,0:T(8,128)(2,1)S(1)} %get-tuple-element.31, ...), kind=kLoop, calls=%fused_computation.8 | loop fusion | flops 124256256 | bytes 70146048 | tf_op jit(solution)/shard_map/convert_element_type | solution.py:33
  68.9 8.6 %copy.28 = bf16[16,64,1536]{1,0,2:T(8,128)(2,1)} copy(bf16[16,64,1536]{2,1,0:T(8,128)(2,1)} %add_convert_fusion) | data formatting | bytes 6291456 | tf_op jit(solution)/shard_map/convert_element_type | solution.py:33
  77.5 9.4 %reshape.56 = bf16[1024,48,32]{0,2,1:T(8,128)(2,1)} reshape(bf16[16,64,1536]{1,0,2:T(8,128)(2,1)} %copy.28) | data formatting | bytes 6291456 | tf_op jit(solution)/shard_map/reshape | solution.py:33
  86.9 2.8 %convolution_convert_fusion.1 = bf16[48,1024,32]{1,2,0:T(8,128)(2,1)S(1)} fusion(bf16[48,32,32]{1,2,0:T(8,128)(2,1)S(1)} %copy.29, bf16[1024,48,32]{0,2,1:T(8,128)(2,1)} %reshape.56), kind=kOutput, calls=%fused_computation.25 | convolution fusion | flops 102236160 | bytes 6389760 | tf_op jit(solution)/shard_map/ngc,gcd->ngd/dot_general | solution.py:34
  89.7 1.1 fusion.15
  90.8 0.8 copy-done.4
  91.6 5.6 %fusion.12 = (f32[1024,16,32]{0,2,1:T(8,128)}, f32[16,32]{1,0:T(8,128)S(1)}, f32[16,32]{1,0:T(8,128)S(1)}, f32[1024,16,32]{0,2,1:T(8,128)}) fusion(bf16[1024,16,3,32]{0,3,2,1:T(8,128)(2,1)S(1)} %bitcast.78, bf16[1024,16,3,32]{0,3,2,1:T(8,128)(2,1)S(1)} %bitcast.80), kind=kLoop, calls=%fused_computation.33 | loop fusion | flops 13630464 | bytes 8392704 | tf_op jit(solution)/shard_map/add | solution.py:23
  97.2 0.8 pad_maximum_fusion.8
  98.1 9.5 %psum.30 = f32[32,32]{1,0:T(8,128)S(1)} all-reduce(f32[32,32]{1,0:T(8,128)S(1)} %pad_maximum_fusion.12), channel_id=1, replica_groups=mesh['groups'=2,'rows'=4,'cols'=4] {'cols'}, use_global_device_ids=true, to_apply=%region_4.5 | all-reduce | flops 1024 | bytes 8192 | tf_op jit(solution)/shard_map/psum | solution.py:61
  107.6 13.8 %psum.31 = f32[32,32]{1,0:T(8,128)S(1)} all-reduce(f32[32,32]{1,0:T(8,128)S(1)} %psum.30), channel_id=1, replica_groups=mesh['groups'=2,'rows'=4,'cols'=4] {'rows'}, use_global_device_ids=true, to_apply=%region_5.6 | all-reduce | flops 1024 | bytes 8192 | tf_op jit(solution)/shard_map/psum | solution.py:60
  121.4 7.7 %all-reduce.3.cloned.1.call-done = f32[32,32,32]{2,1,0:T(8,128)} async-done(((f32[32,32,32]{2,1,0:T(8,128)}), f32[32,32,32]{2,1,0:T(8,128)}) %all-reduce.3.cloned.1.call-update) | async-done | bytes 131088 | tf_op jit(solution)/shard_map/psum | solution.py:61
  129.1 4.3 %fusion.1 = f32[32,1,1024]{2,1,0:T(1,128)S(1)} fusion(f32[32,32,1]{1,2,0:T(1,128)S(1)} %bitcast.84, f32[1024,16,32]{0,2,1:T(8,128)} %get-tuple-element.41, f32[1024,16,32]{0,2,1:T(8,128)} %get-tuple-element.34), kind=kOutput, calls=%fused_computation.19 | convolution fusion | flops 13631488 | bytes 4329472 | tf_op jit(solution)/shard_map/nhd,hd->nh/dot_general | solution.py:78
  133.5 36.8 %all-reduce.5.cloned.1.call-done = f32[32,32,32]{2,1,0:T(8,128)} async-done(((f32[32,32,32]{2,1,0:T(8,128)}), f32[32,32,32]{2,1,0:T(8,128)}) %all-reduce.5.cloned.1.call-update) | async-done | bytes 131088 | tf_op jit(solution)/shard_map/psum | solution.py:60
  170.3 5.7 %fusion = bf16[1024,32,32]{0,2,1:T(8,128)(2,1)S(1)} fusion(f32[1024,32]{0,1:T(8,128)S(1)} %bitcast.83, f32[32,32,32]{2,1,0:T(8,128)} %all-reduce.5.cloned.1.call-done, f32[1024,16,32]{0,2,1:T(8,128)} %get-tuple-element.41, f32[1024,16,32]{0,2,1:T(8,128)} %get-tuple-element.34), kind=kOutput, calls=%fused_computation.13 | convolution fusion | flops 405798912 | bytes 6553600 | tf_op jit(solution)/shard_map/nhd,hde->nhe/dot_general | solution.py:77
  176.1 2.3 %add_convert_fusion.1 = bf16[1024,512]{1,0:T(8,128)(2,1)} fusion(bf16[1024,512]{1,0:T(8,128)(2,1)S(1)} %bitcast.86, bf16[1024,1024]{0,1:T(8,128)(2,1)S(1)} %bitcast.87, bf16[1024,512]{1,0:T(8,128)(2,1)S(1)} %copy-done.22, f32[512]{0:T(512)S(1)} %copy-done.23, f32[512]{0:T(512)S(1)} %copy-done.24), kind=kOutput, calls=%fused_computation.36 | convolution fusion | flops 1076363264 | bytes 5246976 | tf_op jit(solution)/shard_map/dot_general | solution.py:82
  (55 shorter events, 0.2 us)
Async XLA Ops:
  6.5 1.4 copy-start
  6.5 122.6 %all-reduce.3.cloned.1.call-start = ((), (), s32[]{:S(2)}) async-start(), calls=%async_computation | async-start | bytes 1048576 | tf_op jit(solution)/shard_map/psum | solution.py:61
  11.0 1.7 copy-start.1
  12.7 13.6 %collective-permute-start = (bf16[2,64,1536]{2,1,0:T(8,128)(2,1)S(1)}, bf16[2,64,1536]{2,1,0:T(8,128)(2,1)S(1)}, u32[]{:S(2)}, u32[]{:S(2)}) collective-permute-start(bf16[2,64,1536]{2,1,0:T(8,128)(2,1)S(1)} %bitcast.82), channel_id=1, source_target_pairs={{0,4},{4,8},{8,12},{1,5},{5,9},{9,13},{2,6},{6,10},{10,14},{3,7},{... | collective-permute-start | bytes 1179656 | tf_op jit(solution)/shard_map/ppermute | solution.py:16
  16.7 11.6 %collective-permute-start.1 = (bf16[2,64,1536]{2,1,0:T(8,128)(2,1)S(1)}, bf16[2,64,1536]{2,1,0:T(8,128)(2,1)S(1)}, u32[]{:S(2)}, u32[]{:S(2)}) collective-permute-start(bf16[2,64,1536]{2,1,0:T(8,128)(2,1)S(1)} %bitcast.81), channel_id=1, source_target_pairs={{4,0},{8,4},{12,8},{5,1},{9,5},{13,9},{6,2},{10,6},{14,10},{7,3},{... | collective-permute-start | bytes 1179656 | tf_op jit(solution)/shard_map/ppermute | solution.py:17
  22.8 5.5 %copy-start.2 = (bf16[1024,1536]{1,0:T(8,128)(2,1)S(1)}, bf16[1024,1536]{1,0:T(8,128)(2,1)}, u32[]{:S(2)}) copy-start(bf16[1024,1536]{1,0:T(8,128)(2,1)} %copy-done.1) | copy-start | bytes 9437188
  22.8 12.7 %copy-start.7 = (f32[25,1536]{1,0:T(8,128)S(1)}, f32[25,1536]{1,0:T(8,128)}, u32[]{:S(2)}) copy-start(f32[25,1536]{1,0:T(8,128)} %param.9) | copy-start | bytes 460804
  22.8 13.6 %copy-start.5 = (bf16[48,32,32]{0,2,1:T(8,128)(2,1)S(1)}, bf16[48,32,32]{0,2,1:T(8,128)(2,1)}, u32[]{:S(2)}) copy-start(bf16[48,32,32]{0,2,1:T(8,128)(2,1)} %param.10) | copy-start | bytes 294916
  28.5 9.8 %collective-permute-start.2 = (bf16[20,2,1536]{2,1,0:T(2,128)(2,1)S(1)}, bf16[20,2,1536]{2,1,0:T(2,128)(2,1)S(1)}, u32[]{:S(2)}, u32[]{:S(2)}) collective-permute-start(bf16[20,2,1536]{2,1,0:T(2,128)(2,1)S(1)} %get-tuple-element.32), channel_id=1, source_target_pairs={{0,1},{1,2},{2,3},{4,5},{5,6},{6,7},{8,9},{9,10},{10,11},{12,13},{... | collective-permute-start | bytes 368648 | tf_op jit(solution)/shard_map/ppermute | solution.py:16
  33.4 6.2 %collective-permute-start.3 = (bf16[20,2,1536]{2,1,0:T(2,128)(2,1)S(1)}, bf16[20,2,1536]{2,1,0:T(2,128)(2,1)S(1)}, u32[]{:S(2)}, u32[]{:S(2)}) collective-permute-start(bf16[20,2,1536]{2,1,0:T(2,128)(2,1)S(1)} %get-tuple-element.33), channel_id=1, source_target_pairs={{1,0},{2,1},{3,2},{5,4},{6,5},{7,6},{9,8},{10,9},{11,10},{13,12},{... | collective-permute-start | bytes 368648 | tf_op jit(solution)/shard_map/ppermute | solution.py:17
  38.2 6.5 %copy-start.3 = (bf16[1024,1536]{1,0:T(8,128)(2,1)S(1)}, bf16[1024,1536]{1,0:T(8,128)(2,1)}, u32[]{:S(2)}) copy-start(bf16[1024,1536]{1,0:T(8,128)(2,1)} %copy-done.1) | copy-start | bytes 9437188
  38.2 6.5 %copy-start.8 = (f32[1536]{0:T(1024)S(1)}, f32[1536]{0:T(1024)}, u32[]{:S(2)}) copy-start(f32[1536]{0:T(1024)} %get-tuple-element.11) | copy-start | bytes 18436
  38.2 6.5 %copy-start.9 = (f32[1536]{0:T(1024)S(1)}, f32[1536]{0:T(1024)}, u32[]{:S(2)}) copy-start(f32[1536]{0:T(1024)} %get-tuple-element.12) | copy-start | bytes 18436
  38.2 6.5 %copy-start.10 = (f32[1536]{0:T(1024)S(1)}, f32[1536]{0:T(1024)}, u32[]{:S(2)}) copy-start(f32[1536]{0:T(1024)} %get-tuple-element.13) | copy-start | bytes 18436
  38.2 6.5 %copy-start.11 = (f32[1536]{0:T(1024)S(1)}, f32[1536]{0:T(1024)}, u32[]{:S(2)}) copy-start(f32[1536]{0:T(1024)} %get-tuple-element.14) | copy-start | bytes 18436
  38.3 6.5 %copy-start.12 = (f32[1536]{0:T(1024)S(1)}, f32[1536]{0:T(1024)}, u32[]{:S(2)}) copy-start(f32[1536]{0:T(1024)} %get-tuple-element.15) | copy-start | bytes 18436
  38.3 6.5 %copy-start.13 = (f32[1536]{0:T(1024)S(1)}, f32[1536]{0:T(1024)}, u32[]{:S(2)}) copy-start(f32[1536]{0:T(1024)} %get-tuple-element.16) | copy-start | bytes 18436
  38.3 6.5 %copy-start.14 = (f32[1536]{0:T(1024)S(1)}, f32[1536]{0:T(1024)}, u32[]{:S(2)}) copy-start(f32[1536]{0:T(1024)} %get-tuple-element.17) | copy-start | bytes 18436
  38.3 6.5 %copy-start.15 = (f32[1536]{0:T(1024)S(1)}, f32[1536]{0:T(1024)}, u32[]{:S(2)}) copy-start(f32[1536]{0:T(1024)} %get-tuple-element.18) | copy-start | bytes 18436
  38.3 6.5 %copy-start.16 = (f32[1536]{0:T(1024)S(1)}, f32[1536]{0:T(1024)}, u32[]{:S(2)}) copy-start(f32[1536]{0:T(1024)} %get-tuple-element.19) | copy-start | bytes 18436
  38.3 6.5 %copy-start.17 = (f32[1536]{0:T(1024)S(1)}, f32[1536]{0:T(1024)}, u32[]{:S(2)}) copy-start(f32[1536]{0:T(1024)} %get-tuple-element.20) | copy-start | bytes 18436
  38.3 6.5 %copy-start.18 = (f32[1536]{0:T(1024)S(1)}, f32[1536]{0:T(1024)}, u32[]{:S(2)}) copy-start(f32[1536]{0:T(1024)} %get-tuple-element.21) | copy-start | bytes 18436
  38.3 6.5 %copy-start.19 = (f32[1536]{0:T(1024)S(1)}, f32[1536]{0:T(1024)}, u32[]{:S(2)}) copy-start(f32[1536]{0:T(1024)} %get-tuple-element.22) | copy-start | bytes 18436
  38.3 6.5 %copy-start.20 = (f32[1536]{0:T(1024)S(1)}, f32[1536]{0:T(1024)}, u32[]{:S(2)}) copy-start(f32[1536]{0:T(1024)} %get-tuple-element.23) | copy-start | bytes 18436
  89.7 1.9 %copy-start.4 = (bf16[1024,1536]{0,1:T(8,128)(2,1)S(1)}, bf16[1024,1536]{0,1:T(8,128)(2,1)}, u32[]{:S(2)}) copy-start(bf16[1024,1536]{0,1:T(8,128)(2,1)} %copy.26) | copy-start | bytes 9437188
  91.6 5.6 %copy-start.6 = (f32[16,32,32]{2,1,0:T(8,128)S(1)}, f32[16,32,32]{2,1,0:T(8,128)}, u32[]{:S(2)}) copy-start(f32[16,32,32]{2,1,0:T(8,128)} %fusion.16) | copy-start | bytes 196612
  98.0 72.2 %all-reduce.5.cloned.1.call-start = ((), (), s32[]{:S(2)}) async-start(), calls=%async_computation.1 | async-start | bytes 1048576 | tf_op jit(solution)/shard_map/psum | solution.py:60
  170.3 5.8 %copy-start.21 = (bf16[16,64,512]{2,1,0:T(8,128)(2,1)S(1)}, bf16[16,64,512]{2,1,0:T(8,128)(2,1)}, u32[]{:S(2)}) copy-start(bf16[16,64,512]{2,1,0:T(8,128)(2,1)} %param.7) | copy-start | bytes 3145732
  170.3 5.8 %copy-start.22 = (bf16[1024,512]{1,0:T(8,128)(2,1)S(1)}, bf16[1024,512]{1,0:T(8,128)(2,1)}, u32[]{:S(2)}) copy-start(bf16[1024,512]{1,0:T(8,128)(2,1)} %param.11) | copy-start | bytes 3145732
  170.3 5.8 %copy-start.23 = (f32[512]{0:T(512)S(1)}, f32[512]{0:T(512)}, u32[]{:S(2)}) copy-start(f32[512]{0:T(512)} %param.13) | copy-start | bytes 6148
  170.3 5.8 %copy-start.24 = (f32[512]{0:T(512)S(1)}, f32[512]{0:T(512)}, u32[]{:S(2)}) copy-start(f32[512]{0:T(512)} %param.12) | copy-start | bytes 6148
Sparse Core Ops, SparseCore 0:
  98.2 30.8 all-reduce.2
  131.4 38.7 all-reduce.4
